TPU v7x, 512 devices: a whole 4x8x8 slice. The times are simulated.
512 devices in a mesh: band: 8 (over y), gy: 8 (over z), gz: 8 (over x, core).
Axes of the slice: x: 4, y: 8, z: 8, core: 2. Of those that a mesh axis runs over, the one named last changes fastest.
Arguments:
- orbitals: float32 [1024, 48, 3840], P('band', 'gy', 'gz'), may hold values from -6 to 6
- occupied: bfloat16 [1024, 48, 3840], P('band', 'gy', 'gz'), may hold values from -6 to 6
- eigen: float32 [1024], P('band'), may hold values from -1.5 to 0
- potential: float32 [48, 3840], P('gy', 'gz'), may hold values from -2 to 0.5
- perturbation: float32 [48, 3840], P('gy', 'gz'), may hold values from 0.2 to 1.5
- precondition: float32 [48, 3840], P('gy', 'gz'), may hold values from 0.05 to 0.3
Outputs:
- updated: float32 [1024, 48, 3840], P('band', 'gy', 'gz')
- resid_norm: float32 [1024], P('band')
All inputs are finite; a program needn't handle non-finite values.
Results may differ from a plain program's by a relative error of at most 0.0008.
Values may be sent and summed in bfloat16 or wider, within the bound.
A program may use at most 128 MiB of HBM per device.

v0:
```python
import jax
import jax.numpy as jnp
from jax import lax
from jax.sharding import PartitionSpec as P

NX = 80


stencil = (-205.0 / 72.0, 8.0 / 5.0, -1.0 / 5.0, 8.0 / 315.0, -1.0 / 560.0)


def extended(block, sides, width):
    for axis, dim in sides:
        count = lax.axis_size(axis)
        forward = [(i, i + 1) for i in range(count - 1)]
        forward.append((count - 1, 0))
        backward = [(target, source) for source, target in forward]
        low = lax.ppermute(
            lax.slice_in_dim(block, block.shape[dim] - width, None, axis=dim), axis, forward
        )
        high = lax.ppermute(lax.slice_in_dim(block, 0, width, axis=dim), axis, backward)
        block = jnp.concatenate([low, block, high], axis=dim)
    return block


def along_x(field, dist):
    flat = field.shape[-1]
    position = lax.broadcasted_iota(jnp.int32, (flat,), 0) % NX
    lower = jnp.where(position >= dist, jnp.roll(field, dist, -1), jnp.roll(field, dist - NX, -1))
    upper = jnp.where(
        position < NX - dist, jnp.roll(field, -dist, -1), jnp.roll(field, NX - dist, -1)
    )
    return lower + upper


def laplace(field):
    rows_y = field.shape[1]
    flat = field.shape[2]
    padded_y = extended(field, (("gy", 1),), 4)
    padded_z = extended(field, (("gz", 2),), 4 * NX)
    total = 3.0 * stencil[0] * field
    for dist in range(1, 5):
        pair_y = (
            padded_y[:, 4 + dist : 4 + dist + rows_y, :]
            + padded_y[:, 4 - dist : 4 - dist + rows_y, :]
        )
        pair_z = (
            padded_z[:, :, (4 + dist) * NX : (4 + dist) * NX + flat]
            + padded_z[:, :, (4 - dist) * NX : (4 - dist) * NX + flat]
        )
        total = total + stencil[dist] * (along_x(field, dist) + pair_y + pair_z)
    return total


def on_device(orbitals, occupied, eigen, potential, perturbation, precondition):
    band_rows, rows_y, flat = orbitals.shape
    cells = NX * rows_y * lax.axis_size("gy") * (flat // NX) * lax.axis_size("gz")
    occ_wide = occupied.astype(jnp.float32)
    resid = (
        -0.5 * laplace(orbitals)
        + (potential[None] - eigen[:, None, None]) * orbitals
        + perturbation[None] * occ_wide
    )
    squares = jnp.sum(resid * resid, axis=(1, 2))
    squares = lax.psum(squares, ("gy", "gz"))
    trial = orbitals - precondition[None] * resid
    trial_low = trial.astype(jnp.bfloat16)
    partial_margins = jnp.einsum(
        "oyc,ryc->or",
        lax.all_gather(occupied, "band", axis=0, tiled=True),
        trial_low,
        preferred_element_type=jnp.float32,
    )
    margins = lax.psum(partial_margins, ("gy", "gz"))
    norms = jnp.sqrt(squares / cells + 1e-06)
    coeff = (margins / cells).astype(jnp.bfloat16)
    correction = jnp.einsum(
        "or,oyc->ryc",
        coeff,
        lax.all_gather(occupied, "band", axis=0, tiled=True),
        preferred_element_type=jnp.float32,
    )
    updated = trial - correction
    return (updated, norms)


def solution(mesh):
    placed = (
        P("band", "gy", "gz"),
        P("band", "gy", "gz"),
        P("band"),
        P("gy", "gz"),
        P("gy", "gz"),
        P("gy", "gz"),
    )
    return jax.shard_map(
        on_device,
        mesh=mesh,
        in_specs=placed,
        out_specs=(P("band", "gy", "gz"), P("band")),
        check_vma=False,
    )
```

profile of v0, /device:TPU:1, one launch (start us, length us, event | category | flops | bytes accessed | tf_op | source)
XLA Modules:
  0.0 304.9 jit_solution(4770405374905059568)
XLA Ops:
  7.2 0.7 all-gather.2.cloned.1.call-update
  8.0 1.7 fusion.56
  9.7 4.8 %collective-permute-start.1 = (f32[128,4,480]{0,2,1:T(8,128)S(1)}, f32[128,4,480]{0,2,1:T(8,128)S(1)}, u32[]{:S(2)}, u32[]{:S(2)}) collective-permute-start(f32[128,4,480]{0,2,1:T(8,128)S(1)} %get-tuple-element.37), channel_id=1, source_target_pairs={{0,8},{8,16},{16,24},{24,32},{32,40},{40,48},{48,56},{56,0},{1,9},... | collective-permute-start | bytes 2949128 | tf_op jit(solution)/shard_map/ppermute | solution.py:18
  14.5 0.2 fusion.57
  14.7 2.1 collective-permute-start.3
  16.8 8.3 %collective-permute-start = (f32[128,4,480]{0,2,1:T(8,128)S(1)}, f32[128,4,480]{0,2,1:T(8,128)S(1)}, u32[]{:S(2)}, u32[]{:S(2)}) collective-permute-start(f32[128,4,480]{0,2,1:T(8,128)S(1)} %get-tuple-element.36), channel_id=1, source_target_pairs={{8,0},{16,8},{24,16},{32,24},{40,32},{48,40},{56,48},{0,56},{9,1},... | collective-permute-start | bytes 2949128 | tf_op jit(solution)/shard_map/ppermute | solution.py:21
  25.1 0.6 fusion.40
  25.8 0.8 fusion.47
  26.6 0.8 fusion.51
  27.5 0.9 fusion.55
  28.3 1.2 fusion.46
  29.5 1.6 fusion.50
  31.1 1.9 fusion.45
  33.0 1.9 fusion.49
  34.9 1.8 fusion.53
  36.7 1.8 fusion.41
  38.5 0.5 fusion.29
  39.1 0.6 fusion.31
  39.6 1.6 fusion.54
  41.2 0.6 fusion.33
  41.8 0.5 fusion.35
  42.4 1.6 fusion.42
  44.2 0.6 constant_dynamic-update-slice_fusion.1
  44.8 1.2 collective-permute-done
  46.2 0.6 copy-done.2
  46.8 13.7 %multiply_reduce_fusion = (f32[128]{0:T(128)}, f32[128,6,480]{0,2,1:T(8,128)S(1)}) fusion(bf16[128,6,480]{0,2,1:T(8,128)(2,1)} %param.7, f32[6,480]{1,0:T(8,128)S(1)} %copy-done.2, f32[128,6,480]{0,2,1:T(8,128)S(1)} %copy-done, f32[128]{0:T(128)} %param.8, f32[6,480]{1,0:T(8,128)S(1)} %copy-done.3, f32[128,6,800]{0,2,1:T(8,128)S(1)} %get-tuple-element.39, ...), kind=kLoop, calls=%fused_computation.39 | loop fusion | flops 22855552 | bytes 50900224 | tf_op jit(solution)/shard_map/reduce_sum | solution.py:64
  60.5 31.8 %all-gather.2.cloned.1.call-done = bf16[1024,6,480]{0,2,1:T(8,128)(2,1)} async-done(((bf16[128,6,480]{0,2,1:T(8,128)(2,1)}), bf16[1024,6,480]{0,2,1:T(8,128)(2,1)}) %all-gather.2.cloned.1.call-update) | async-done | bytes 5898256 | tf_op jit(solution)/shard_map/all_gather | solution.py:70
  92.4 6.2 %convolution_bitcast_fusion = f32[1024,128]{1,0:T(8,128)} fusion(bf16[1024,6,480]{0,2,1:T(8,128)(2,1)} %all-gather.2.cloned.1.call-done, f32[128,6,480]{0,2,1:T(8,128)S(1)} %copy-done, f32[128,6,480]{0,2,1:T(8,128)S(1)} %get-tuple-element.3, f32[6,480]{1,0:T(8,128)S(1)} %copy-done.1), kind=kOutput, calls=%fused_computation.42 | convolution fusion | flops 756080640 | bytes 9383168 | tf_op jit(solution)/shard_map/oyc,ryc->or/dot_general | solution.py:68
  98.7 128.5 %psum.15 = f32[128]{0:T(128)S(1)} all-reduce(f32[128]{0:T(128)S(1)} %copy-done.4), channel_id=1, replica_groups=mesh['band'=8,'gy'=8,'gz'=8] {'gy','gz'}, use_global_device_ids=true, to_apply=%region_2.3 | all-reduce | flops 128 | bytes 1024 | tf_op jit(solution)/shard_map/psum | solution.py:65
  227.1 0.5 add_sqrt_fusion
  227.6 64.8 %all-reduce.2.cloned.1.call-done = f32[1024,128]{1,0:T(8,128)} async-done(((f32[1024,128]{1,0:T(8,128)}), f32[1024,128]{1,0:T(8,128)}) %all-reduce.2.cloned.1.call-update) | async-done | bytes 524304 | tf_op jit(solution)/shard_map/psum | solution.py:74
  292.4 5.7 %convolution_subtract_fusion = f32[128,6,480]{0,2,1:T(8,128)} fusion(bf16[1024,6,480]{0,2,1:T(8,128)(2,1)} %all-gather.2.cloned.1.call-done, f32[128,6,480]{0,2,1:T(8,128)S(1)} %copy-done, f32[128,6,480]{0,2,1:T(8,128)S(1)} %get-tuple-element.3, f32[6,480]{1,0:T(8,128)S(1)} %copy-done.1, f32[1024,128]{1,0:T(8,128)} %all-reduce.2.cloned.1.call-done), kind=kOutput, calls=%fused_computation.41 | convolution fusion | flops 756342784 | bytes 10857728 | tf_op jit(solution)/shard_map/or,oyc->ryc/dot_general | solution.py:77
  (24 shorter events, 0.5 us)
Async XLA Ops:
  7.2 85.2 %all-gather.2.cloned.1.call-start = ((), (), s32[]{:S(2)}) async-start(), calls=%async_computation | async-start | bytes 6635520 | tf_op jit(solution)/shard_map/all_gather | solution.py:70
  7.9 6.6 %copy-start = (f32[128,6,480]{0,2,1:T(8,128)S(1)}, f32[128,6,480]{0,2,1:T(8,128)}, u32[]{:S(2)}) copy-start(f32[128,6,480]{0,2,1:T(8,128)} %param.6) | copy-start | bytes 4423684
  7.9 284.5 %all-reduce.2.cloned.1.call-start = ((), (), s32[]{:S(2)}) async-start(), calls=%async_computation.1 | async-start | bytes 1048576 | tf_op jit(solution)/shard_map/psum | solution.py:74
  9.7 34.3 %collective-permute-start.1 = (f32[128,4,480]{0,2,1:T(8,128)S(1)}, f32[128,4,480]{0,2,1:T(8,128)S(1)}, u32[]{:S(2)}, u32[]{:S(2)}) collective-permute-start(f32[128,4,480]{0,2,1:T(8,128)S(1)} %get-tuple-element.37), channel_id=1, source_target_pairs={{0,8},{8,16},{16,24},{24,32},{32,40},{40,48},{48,56},{56,0},{1,9},... | collective-permute-start | bytes 2949128 | tf_op jit(solution)/shard_map/ppermute | solution.py:18
  14.7 29.4 %collective-permute-start.3 = (f32[128,6,320]{0,2,1:T(8,128)S(1)}, f32[128,6,320]{0,2,1:T(8,128)S(1)}, u32[]{:S(2)}, u32[]{:S(2)}) collective-permute-start(f32[128,6,320]{0,2,1:T(8,128)S(1)} %get-tuple-element.43), channel_id=1, source_target_pairs={{0,1},{1,2},{2,3},{3,4},{4,5},{5,6},{6,7},{7,0},{8,9},{9,10},{10,1... | collective-permute-start | bytes 2949128 | tf_op jit(solution)/shard_map/ppermute | solution.py:18
  16.8 29.2 %collective-permute-start = (f32[128,4,480]{0,2,1:T(8,128)S(1)}, f32[128,4,480]{0,2,1:T(8,128)S(1)}, u32[]{:S(2)}, u32[]{:S(2)}) collective-permute-start(f32[128,4,480]{0,2,1:T(8,128)S(1)} %get-tuple-element.36), channel_id=1, source_target_pairs={{8,0},{16,8},{24,16},{32,24},{40,32},{48,40},{56,48},{0,56},{9,1},... | collective-permute-start | bytes 2949128 | tf_op jit(solution)/shard_map/ppermute | solution.py:21
  25.1 21.0 %collective-permute-start.2 = (f32[128,6,320]{0,2,1:T(8,128)S(1)}, f32[128,6,320]{0,2,1:T(8,128)S(1)}, u32[]{:S(2)}, u32[]{:S(2)}) collective-permute-start(f32[128,6,320]{0,2,1:T(8,128)S(1)} %get-tuple-element.42), channel_id=1, source_target_pairs={{1,0},{2,1},{3,2},{4,3},{5,4},{6,5},{7,6},{0,7},{9,8},{10,9},{11,1... | collective-permute-start | bytes 2949128 | tf_op jit(solution)/shard_map/ppermute | solution.py:21
  46.1 0.7 copy-start.2
  46.1 0.7 copy-start.3
  46.8 45.5 %copy-start.1 = (f32[6,480]{1,0:T(8,128)S(1)}, f32[6,480]{1,0:T(8,128)}, u32[]{:S(2)}) copy-start(f32[6,480]{1,0:T(8,128)} %param.11) | copy-start | bytes 34564
  92.4 6.3 %copy-start.4 = (f32[128]{0:T(128)S(1)}, f32[128]{0:T(128)}, u32[]{:S(2)}) copy-start(f32[128]{0:T(128)} %get-tuple-element.2) | copy-start | bytes 1540
Sparse Core Ops, SparseCore 0:
  10.0 82.3 all-gather.1
  98.8 193.6 all-reduce.1
where the time goes:
time: 306 us; the launch traced here: 305 us
  blocking collectives  128 us (42%)
  waiting for transfers between devices  98.5 us (32%)
  local copies, waits for them, and re-layouts  20.1 us (7%)
  other arithmetic  16.5 us (5%)
  starting transfers between devices  15.3 us (5%)
  between operations  14.2 us (5%)
  matrix products  11.9 us (4%)
    psum x1, blocking collectives, on_device(): squares = lax.psum(squares, ('gy', 'gz'))  128 us
    psum x1, waiting for transfers between devices, on_device(): margins = lax.psum(partial_margins, ('gy', 'gz'))  64.8 us
    all_gather x1, waiting for transfers between devices, on_device(): lax.all_gather(occupied, 'band', axis=0, tiled=True)  31.8 us
    reduce_sum x1, other arithmetic, on_device(): squares = jnp.sum(resid * resid, axis=(1, 2))  13.7 us
    slice x8, local copies, waits for them, and re-layouts, along_x(): jnp.roll(field, dist - NX, -1)  8.63 us
    ppermute x2, starting transfers between devices, extended(): lax.ppermute(lax.slice_in_dim(block, 0, width, axis=dim), axis, backward)  8.31 us
    slice x8, local copies, waits for them, and re-layouts, along_x(): jnp.roll(field, dist, -1)  8.01 us
    ppermute x2, starting transfers between devices, extended(): lax.ppermute(lax.slice_in_dim(block, block.shape[dim] - width, None, axis...  6.89 us
  transfers between devices with their start and end apart: 6, of which 3 were waited for; matrix products, arithmetic and copies ran while one was open for 12% of the time, Pallas kernels for 0%

commit v1 on v0

v1 whole, which is shorter than its diff:
```python
import functools
import jax
import jax.numpy as jnp
from jax import lax
from jax.experimental import pallas as pl
from jax.experimental.pallas import tpu as pltpu
from jax.sharding import PartitionSpec as P

NX = 80
REACH = 4
MESH = pl.DeviceIdType.MESH

stencil = (-205.0 / 72.0, 8.0 / 5.0, -1.0 / 5.0, 8.0 / 315.0, -1.0 / 560.0)


def ring_plan(groups):
    far = groups // 2
    plans = []
    for order in ((0, 1, 2, 3), (2, 3, 0, 1)):
        plan = [(k, c) for k in range(1, far) for c in order]
        plan += [(far, c) for c in order[:2]]
        plans.append(plan)
    return plans


def round_plan(groups):
    far = groups // 2
    rounds = [[0, 1, groups - 1]] if far > 1 else [[0]]
    rounds += [[k, groups - k] for k in range(2, far)]
    rounds += [[far]]
    return rounds


def kernel(
    nb, ny, nz, total_cells,
    psi_hbm, occ_hbm, eig_ref, pot_ref, per_ref, pre_ref,
    out_hbm, norm_ref,
    py, pz, fields, occ, trial, low_t, part, rs, gyb, coeff, sq_z, sq_y,
    load_sem, halo_send, halo_recv, ring_send, ring_recv,
    red_send, red_recv, sq_send, sq_recv, out_sem,
):
    rows_y, flat, bands = psi_hbm.shape
    rows_z = flat // NX
    cells = rows_y * flat
    padded = occ.shape[1]
    wide = REACH * NX
    my_b = lax.axis_index("band")
    my_y = lax.axis_index("gy")
    my_z = lax.axis_index("gz")
    sends = []

    def remote(src, dst, send, recv, **where):
        copy = pltpu.make_async_remote_copy(
            src_ref=src, dst_ref=dst, send_sem=send, recv_sem=recv,
            device_id=where, device_id_type=MESH,
        )
        copy.start()
        sends.append(copy)
        return copy

    loads = [
        pltpu.make_async_copy(occ_hbm, occ.at[0, pl.ds(0, cells)], load_sem.at[0]),
        pltpu.make_async_copy(psi_hbm, py.at[pl.ds(REACH, rows_y)], load_sem.at[1]),
        pltpu.make_async_copy(psi_hbm, pz.at[:, pl.ds(wide, flat)], load_sem.at[2]),
    ]
    for load in loads:
        load.start()
    barrier = pltpu.get_barrier_semaphore()
    greeted = 0
    for axis, me, count, steps in (
        ("band", my_b, nb, (1, nb - 1)),
        ("gy", my_y, ny, range(1, ny)),
        ("gz", my_z, nz, range(1, nz)),
    ):
        for step in steps:
            pl.semaphore_signal(
                barrier, inc=1, device_id={axis: lax.rem(me + step, count)}, device_id_type=MESH
            )
            greeted += 1
    pl.semaphore_wait(barrier, greeted)

    plans = ring_plan(nb)
    toward = (lax.rem(my_b + 1, nb), lax.rem(my_b + nb - 1, nb))
    quarter = cells // 4
    ring = [[], []]

    def slot(way, k):
        return k if way == 0 else nb - k

    def ring_start(way, entry):
        k, c = plans[way][entry]
        span = pl.ds(c * quarter, quarter)
        src = occ_hbm.at[span] if k == 1 else occ.at[slot(way, k - 1), span]
        ring[way].append(
            remote(
                src, occ.at[slot(way, k), span],
                ring_send.at[way, entry], ring_recv.at[way, entry], band=toward[way],
            )
        )

    entries = len(plans[0])
    own = min(4, entries)
    for entry in range(own):
        for way in range(2):
            ring_start(way, entry)

    y_up, y_down = lax.rem(my_y + 1, ny), lax.rem(my_y + ny - 1, ny)
    z_up, z_down = lax.rem(my_z + 1, nz), lax.rem(my_z + nz - 1, nz)
    halos = [
        remote(psi_hbm.at[pl.ds(rows_y - REACH, REACH)], py.at[pl.ds(0, REACH)],
               halo_send.at[0], halo_recv.at[0], gy=y_up),
        remote(psi_hbm.at[pl.ds(0, REACH)], py.at[pl.ds(REACH + rows_y, REACH)],
               halo_send.at[1], halo_recv.at[1], gy=y_down),
        remote(psi_hbm.at[:, pl.ds(flat - wide, wide)], pz.at[:, pl.ds(0, wide)],
               halo_send.at[2], halo_recv.at[2], gz=z_up),
        remote(psi_hbm.at[:, pl.ds(0, wide)], pz.at[:, pl.ds(wide + flat, wide)],
               halo_send.at[3], halo_recv.at[3], gz=z_down),
    ]

    arrived = 0

    def advance(upto):
        nonlocal arrived
        while arrived < min(upto, entries):
            for way in range(2):
                ring[way][arrived].wait_recv()
                if arrived + own < entries:
                    ring_start(way, arrived + own)
            arrived += 1

    if padded > cells:
        for at in range(nb):
            occ[at, cells:, :] = jnp.zeros((padded - cells, bands), occ.dtype)
        trial[cells:, :] = jnp.zeros((padded - cells, bands), trial.dtype)
    for at, ref in enumerate((pot_ref, per_ref, pre_ref)):
        columns = jnp.transpose(ref[...])
        for y in range(rows_y):
            fields[at, y * flat : (y + 1) * flat, :] = jnp.broadcast_to(
                columns[:, y : y + 1], (flat, bands)
            )
    for load in loads:
        load.wait()

    advance(4)
    for halo in halos:
        halo.wait_recv()

    energy = eig_ref[...]

    def pencil(at, squares):
        y, z = lax.div(at, rows_z), lax.rem(at, rows_z)
        base = pl.multiple_of(z * NX, 16)
        here = pl.ds(base, NX)
        row = pl.ds(pl.multiple_of(at * NX, 16), NX)
        mid = py[y + REACH, here, :]
        total = (3.0 * stencil[0]) * mid
        for dist in range(1, REACH + 1):
            pair = pltpu.roll(mid, dist, 0) + pltpu.roll(mid, NX - dist, 0)
            pair += py[y + REACH + dist, here, :] + py[y + REACH - dist, here, :]
            pair += (
                pz[y, pl.ds(pl.multiple_of(base + (REACH + dist) * NX, 16), NX), :]
                + pz[y, pl.ds(pl.multiple_of(base + (REACH - dist) * NX, 16), NX), :]
            )
            total += stencil[dist] * pair
        resid = (
            -0.5 * total
            + (fields[0, row, :] - energy) * mid
            + fields[1, row, :] * occ[0, row, :].astype(jnp.float32)
        )
        trial[row, :] = mid - fields[2, row, :] * resid
        return squares + jnp.sum((resid * resid).reshape(NX // 8, 8, bands), axis=0)

    squares = lax.fori_loop(0, rows_y * rows_z, pencil, jnp.zeros((8, bands), jnp.float32))
    advance(5)

    def spread(src, dst_of, sems, axis, me, count):
        copies = []
        for step in range(1, count):
            peer = lax.rem(me + step, count)
            copies.append(
                remote(src(peer), dst_of(peer), red_send.at[sems + (step,)],
                       red_recv.at[sems + (step,)], **{axis: peer})
            )
        return copies

    def arrive(copies):
        for copy in copies:
            copy.wait_recv()

    last = len(round_plan(nb))
    sq_z[my_z] = squares
    sq_copies = spread(lambda p: sq_z.at[my_z], lambda p: sq_z.at[my_z], (last, 0), "gz", my_z, nz)

    for at in range(padded // 128):
        block = pl.ds(at * 128, 128)
        low_t[:, block] = jnp.transpose(trial[block, :]).astype(low_t.dtype)
    advance(6)

    rounds = round_plan(nb)
    starts = [0]
    for group in rounds:
        starts.append(starts[-1] + len(group) * bands)
    share = bands // nz

    def span_of(r):
        return pl.ds(starts[r], starts[r + 1] - starts[r])

    def margins(r):
        for i, at in enumerate(rounds[r]):
            part[:, pl.ds(starts[r] + i * bands, bands)] = jnp.dot(
                low_t[...], occ[at], preferred_element_type=jnp.float32
            )
        cols = span_of(r)
        mine = pl.ds(pl.multiple_of(my_z * share, 16), share)
        copies = spread(
            lambda p: part.at[pl.ds(pl.multiple_of(p * share, 16), share), cols],
            lambda p: rs.at[my_z, :, cols],
            (r, 0), "gz", my_z, nz,
        )
        rs[my_z, :, cols] = part[mine, cols]
        return copies

    def over_y(r, copies):
        arrive(copies)
        cols = span_of(r)
        total = rs[0, :, cols]
        for at in range(1, nz):
            total += rs[at, :, cols]
        gyb[my_y, :, cols] = total
        return spread(
            lambda p: gyb.at[my_y, :, cols], lambda p: gyb.at[my_y, :, cols],
            (r, 1), "gy", my_y, ny,
        )

    def over_z(r, copies):
        arrive(copies)
        cols = span_of(r)
        total = gyb[0, :, cols]
        for at in range(1, ny):
            total += gyb[at, :, cols]
        mine = pl.ds(pl.multiple_of(my_z * share, 16), share)
        coeff[mine, cols] = (total / total_cells).astype(coeff.dtype)
        return spread(
            lambda p: coeff.at[mine, cols], lambda p: coeff.at[mine, cols],
            (r, 2), "gz", my_z, nz,
        )

    def correct(r, copies, finish=None):
        arrive(copies)

        def rows(y, carry):
            row = pl.ds(pl.multiple_of(y * flat, 16), flat)
            total = trial[row, :]
            for i, at in enumerate(rounds[r]):
                total -= lax.dot_general(
                    occ[at, row, :], coeff[:, pl.ds(starts[r] + i * bands, bands)],
                    (((1,), (1,)), ((), ())), preferred_element_type=jnp.float32,
                )
            trial[row, :] = total
            return carry

        if finish is None:
            lax.fori_loop(0, rows_y, rows, 0)
        else:
            for y in range(rows_y):
                rows(y, 0)
                finish(y)

    outs = []

    def finish(y):
        copy = pltpu.make_async_copy(
            trial.at[pl.ds(y * flat, flat)], out_hbm.at[y], out_sem.at[y]
        )
        copy.start()
        outs.append(copy)

    before = None
    for r in range(last):
        dist = r + 1
        advance(4 * dist)
        one = margins(r)
        if r == 0:
            arrive(sq_copies)
            over = sq_z[0]
            for at in range(1, nz):
                over += sq_z[at]
            sq_y[my_y] = over
            sq_copies = spread(
                lambda p: sq_y.at[my_y], lambda p: sq_y.at[my_y], (last, 1), "gy", my_y, ny
            )
        advance(4 * dist + 1)
        if before is not None:
            three = over_z(r - 1, before)
            two = over_y(r, one)
            advance(4 * dist + 2)
            correct(r - 1, three)
        else:
            two = over_y(r, one)
        before = two
    three = over_z(last - 1, before)

    arrive(sq_copies)
    over = sq_y[0]
    for at in range(1, ny):
        over += sq_y[at]
    norm_ref[...] = jnp.sqrt(jnp.sum(over, axis=0, keepdims=True) / total_cells + 1e-06)

    correct(last - 1, three, finish)
    for copy in sends:
        copy.wait_send()
    for copy in outs:
        copy.wait()


def on_device(nb, ny, nz, orbitals, occupied, eigen, potential, perturbation, precondition):
    bands, rows_y, flat = orbitals.shape
    cells = rows_y * flat
    padded = -(-cells // 128) * 128
    total_cells = float(cells * ny * nz)
    psi = jnp.transpose(orbitals, (1, 2, 0))
    occ = jnp.transpose(occupied, (1, 2, 0)).reshape(cells, bands)
    rounds = len(round_plan(nb))
    entries = len(ring_plan(nb)[0])
    share = bands // nz
    everywhere = pl.BlockSpec(memory_space=pl.ANY)
    local = pl.BlockSpec(memory_space=pltpu.VMEM)
    f32, bf16 = jnp.float32, jnp.bfloat16
    dma = pltpu.SemaphoreType.DMA
    updated, norms = pl.pallas_call(
        functools.partial(kernel, nb, ny, nz, total_cells),
        out_shape=(
            jax.ShapeDtypeStruct((rows_y, flat, bands), f32),
            jax.ShapeDtypeStruct((1, bands), f32),
        ),
        in_specs=[everywhere, everywhere, local, local, local, local],
        out_specs=(everywhere, local),
        scratch_shapes=[
            pltpu.VMEM((rows_y + 2 * REACH, flat, bands), f32),
            pltpu.VMEM((rows_y, flat + 2 * REACH * NX, bands), f32),
            pltpu.VMEM((3, cells, bands), f32),
            pltpu.VMEM((nb, padded, bands), bf16),
            pltpu.VMEM((padded, bands), f32),
            pltpu.VMEM((bands, padded), bf16),
            pltpu.VMEM((bands, nb * bands), f32),
            pltpu.VMEM((nz, share, nb * bands), f32),
            pltpu.VMEM((ny, share, nb * bands), f32),
            pltpu.VMEM((bands, nb * bands), bf16),
            pltpu.VMEM((nz, 8, bands), f32),
            pltpu.VMEM((ny, 8, bands), f32),
            dma((3,)), dma((4,)), dma((4,)), dma((2, entries)), dma((2, entries)),
            dma((rounds + 1, 3, max(ny, nz))), dma((rounds + 1, 3, max(ny, nz))),
            dma((1,)), dma((1,)), dma((rows_y,)),
        ],
        compiler_params=pltpu.CompilerParams(
            collective_id=0, has_side_effects=True, vmem_limit_bytes=60 * 1024 * 1024
        ),
        name="sternheimer",
    )(psi, occ, eigen.reshape(1, bands), potential, perturbation, precondition)
    return jnp.transpose(updated, (2, 0, 1)), norms.reshape(bands)


def solution(mesh):
    placed = (
        P("band", "gy", "gz"),
        P("band", "gy", "gz"),
        P("band"),
        P("gy", "gz"),
        P("gy", "gz"),
        P("gy", "gz"),
    )
    sizes = tuple(mesh.shape[axis] for axis in ("band", "gy", "gz"))
    return jax.shard_map(
        functools.partial(on_device, *sizes),
        mesh=mesh,
        in_specs=placed,
        out_specs=(P("band", "gy", "gz"), P("band")),
        check_vma=False,
    )
```

time: 306 us -> 96 us (0.31)
  blocking collectives: 128 us -> 0 us
  waiting for transfers between devices: 98.5 us -> 0 us
  Pallas kernels: 0 us -> 92 us
  local copies, waits for them, and re-layouts: 20.1 us -> 3.09 us
  other arithmetic: 16.5 us -> 0 us
  starting transfers between devices: 15.3 us -> 0 us
  between operations: 14.2 us -> 0.65 us
  matrix products: 11.9 us -> 0 us
    psum x1 -> x0, blocking collectives: 128 us -> none  [on_device(): squares = lax.psum(squares, ('gy', 'gz'))]
    pallas_call x0 -> x1, Pallas kernels: none -> 92 us  [on_device(): pl.pallas_call(functools.partial(kernel, nb, ny, nz, total_cells), out_sh...]
    psum x1 -> x0, waiting for transfers between devices: 64.8 us -> none  [on_device(): margins = lax.psum(partial_margins, ('gy', 'gz'))]
    all_gather x1 -> x0, waiting for transfers between devices: 31.8 us -> none  [on_device(): lax.all_gather(occupied, 'band', axis=0, tiled=True)]
    slice x18 -> x0, local copies, waits for them, and re-layouts: 18.5 us -> none  [the longest x8 8.63 us: along_x(): jnp.roll(field, dist - NX, -1)]
    ppermute x4 -> x0, starting transfers between devices: 15.2 us -> none  [the longest x2 8.31 us: extended(): lax.ppermute(lax.slice_in_dim(block, 0, width, axis=dim), axis, backward)]
    reduce_sum x1 -> x0, other arithmetic: 13.7 us -> none  [on_device(): squares = jnp.sum(resid * resid, axis=(1, 2))]
    dot_general x2 -> x0, matrix products: 11.9 us -> none  [the longest x1 6.24 us: on_device(): jnp.einsum('oyc,ryc->or', lax.all_gather(occupied, 'band', axis=0, tiled=...]
  transfers between devices with their start and end apart: 6 -> 0, of which waited for: 3 -> 0; matrix products, arithmetic and copies ran while one was open for 12% -> 0% of each run, Pallas kernels for 0% -> 0%
where the time goes in v1:
time: 96 us; the launch traced here: 95.7 us
  Pallas kernels  92 us (96%)
  local copies, waits for them, and re-layouts  3.09 us (3%)
    pallas_call x1, Pallas kernels, on_device(): pl.pallas_call(functools.partial(kernel, nb, ny, nz, total_cells), out_sh...  92 us
    unnamed x4, local copies, waits for them, and re-layouts  3.09 us

profile of v1, /device:TPU:1, one launch (start us, length us, event | category | flops | bytes accessed | tf_op | source)
XLA Modules:
  0.0 95.7 jit_solution(4244136203883153483)
XLA Ops:
  0.6 92.0 %sternheimer.1 = (f32[6,480,128]{2,1,0:T(8,128)}, f32[1,128]{1,0:T(1,128)}) custom-call(f32[6,480,128]{2,1,0:T(8,128)} %bitcast.7, bf16[2880,128]{1,0:T(8,128)(2,1)} %bitcast.9, f32[1,128]{1,0:T(1,128)} %bitcast.10, f32[6,480]{1,0:T(8,128)} %pot_ref.1, f32[6,480]{1,0:T(8,128)} %per_ref.1, f32[6,480]{1,0:T(8,128)} %pre_ref.1), custom_call_target="tpu_custom_call" | custom-call | tf_op jit(solution)/shard_map/sternheimer/pallas_call | solution.py:330
  92.6 0.0 copy-start
  92.6 2.6 %copy.10 = f32[128,6,480]{0,2,1:T(8,128)} copy(f32[128,6,480]{0,2,1:T(8,128)} %bitcast.8) | data formatting | bytes 2949120
  95.2 0.0 copy-done
  95.2 0.5 copy.11
Async XLA Ops:
  92.6 2.6 %copy-start = (f32[1,128]{1,0:T(1,128)S(1)}, f32[1,128]{1,0:T(1,128)}, u32[]{:S(2)}) copy-start(f32[1,128]{1,0:T(1,128)} %get-tuple-element.5) | copy-start | bytes 1540

commit v2 on v1

--- a/solution.py
+++ b/solution.py
@@ -31,13 +31,16 @@
     return rounds
 
 
+def quarters(cells):
+    return [(cells * i // 4 + 64) // 128 * 128 for i in range(4)] + [cells]
+
+
 def kernel(
     nb, ny, nz, total_cells,
     psi_hbm, occ_hbm, eig_ref, pot_ref, per_ref, pre_ref,
-    out_hbm, norm_ref,
-    py, pz, fields, occ, trial, low_t, part, rs, gyb, coeff, sq_z, sq_y,
-    load_sem, halo_send, halo_recv, ring_send, ring_recv,
-    red_send, red_recv, sq_send, sq_recv, out_sem,
+    trial, occ_far, coeff_far, norm_ref,
+    py, pz, fields, occ, low_t, part, rs, gyb, coeff, sq_z, sq_y,
+    load_sem, halo_send, halo_recv, ring_send, ring_recv, red_send, red_recv,
 ):
     rows_y, flat, bands = psi_hbm.shape
     rows_z = flat // NX
@@ -58,13 +61,6 @@
         sends.append(copy)
         return copy
 
-    loads = [
-        pltpu.make_async_copy(occ_hbm, occ.at[0, pl.ds(0, cells)], load_sem.at[0]),
-        pltpu.make_async_copy(psi_hbm, py.at[pl.ds(REACH, rows_y)], load_sem.at[1]),
-        pltpu.make_async_copy(psi_hbm, pz.at[:, pl.ds(wide, flat)], load_sem.at[2]),
-    ]
-    for load in loads:
-        load.start()
     barrier = pltpu.get_barrier_semaphore()
     greeted = 0
     for axis, me, count, steps in (
@@ -77,23 +73,33 @@
                 barrier, inc=1, device_id={axis: lax.rem(me + step, count)}, device_id_type=MESH
             )
             greeted += 1
+    loads = [
+        pltpu.make_async_copy(occ_hbm, occ.at[0, pl.ds(0, cells)], load_sem.at[0]),
+        pltpu.make_async_copy(psi_hbm, py.at[pl.ds(REACH, rows_y)], load_sem.at[1]),
+        pltpu.make_async_copy(psi_hbm, pz.at[:, pl.ds(wide, flat)], load_sem.at[2]),
+    ]
+    for load in loads:
+        load.start()
     pl.semaphore_wait(barrier, greeted)
 
     plans = ring_plan(nb)
     toward = (lax.rem(my_b + 1, nb), lax.rem(my_b + nb - 1, nb))
-    quarter = cells // 4
+    bounds = quarters(cells)
+    far = nb // 2
     ring = [[], []]
 
-    def slot(way, k):
-        return k if way == 0 else nb - k
+    def shard(way, k):
+        if k == far:
+            return occ_far
+        return occ.at[k if way == 0 else nb - k]
 
     def ring_start(way, entry):
         k, c = plans[way][entry]
-        span = pl.ds(c * quarter, quarter)
-        src = occ_hbm.at[span] if k == 1 else occ.at[slot(way, k - 1), span]
+        span = pl.ds(bounds[c], bounds[c + 1] - bounds[c])
+        src = occ_hbm.at[span] if k == 1 else shard(way, k - 1).at[span]
         ring[way].append(
             remote(
-                src, occ.at[slot(way, k), span],
+                src, shard(way, k).at[span],
                 ring_send.at[way, entry], ring_recv.at[way, entry], band=toward[way],
             )
         )
@@ -129,6 +135,7 @@
             arrived += 1
 
     if padded > cells:
+        occ_far[cells:, :] = jnp.zeros((padded - cells, bands), occ.dtype)
         for at in range(nb):
             occ[at, cells:, :] = jnp.zeros((padded - cells, bands), occ.dtype)
         trial[cells:, :] = jnp.zeros((padded - cells, bands), trial.dtype)
@@ -205,12 +212,24 @@
     def span_of(r):
         return pl.ds(starts[r], starts[r + 1] - starts[r])
 
+    def far_margins(chunks):
+        total = 0.0
+        for c in chunks:
+            span = pl.ds(bounds[c], (padded if c == 3 else bounds[c + 1]) - bounds[c])
+            total += jnp.dot(
+                low_t[:, span], occ_far[span, :], preferred_element_type=jnp.float32
+            )
+        return total
+
     def margins(r):
-        for i, at in enumerate(rounds[r]):
-            part[:, pl.ds(starts[r] + i * bands, bands)] = jnp.dot(
-                low_t[...], occ[at], preferred_element_type=jnp.float32
-            )
         cols = span_of(r)
+        if r == last - 1:
+            part[:, cols] += far_margins((1, 3))
+        else:
+            for i, at in enumerate(rounds[r]):
+                part[:, pl.ds(starts[r] + i * bands, bands)] = jnp.dot(
+                    low_t[...], occ[at], preferred_element_type=jnp.float32
+                )
         mine = pl.ds(pl.multiple_of(my_z * share, 16), share)
         copies = spread(
             lambda p: part.at[pl.ds(pl.multiple_of(p * share, 16), share), cols],
@@ -245,7 +264,7 @@
             (r, 2), "gz", my_z, nz,
         )
 
-    def correct(r, copies, finish=None):
+    def correct(r, copies):
         arrive(copies)
 
         def rows(y, carry):
@@ -259,25 +278,14 @@
             trial[row, :] = total
             return carry
 
-        if finish is None:
-            lax.fori_loop(0, rows_y, rows, 0)
-        else:
-            for y in range(rows_y):
-                rows(y, 0)
-                finish(y)
-
-    outs = []
-
-    def finish(y):
-        copy = pltpu.make_async_copy(
-            trial.at[pl.ds(y * flat, flat)], out_hbm.at[y], out_sem.at[y]
-        )
-        copy.start()
-        outs.append(copy)
+        lax.fori_loop(0, rows_y, rows, 0)
 
     before = None
     for r in range(last):
         dist = r + 1
+        if r == last - 1:
+            advance(4 * r + 1)
+            part[:, span_of(r)] = far_margins((0, 2))
         advance(4 * dist)
         one = margins(r)
         if r == 0:
@@ -306,10 +314,25 @@
         over += sq_y[at]
     norm_ref[...] = jnp.sqrt(jnp.sum(over, axis=0, keepdims=True) / total_cells + 1e-06)
 
-    correct(last - 1, three, finish)
+    arrive(three)
+    coeff_far[...] = coeff[:, span_of(last - 1)]
     for copy in sends:
         copy.wait_send()
-    for copy in outs:
+
+
+def far_correction(trial, occ_far, coeff_far, norm_ref, out_hbm, norm_out, held, sems):
+    rows_y, flat, bands = out_hbm.shape
+    norm_out[...] = norm_ref[...]
+    copies = []
+    for y in range(rows_y):
+        row = pl.ds(y * flat, flat)
+        held[row, :] = trial[row, :] - lax.dot_general(
+            occ_far[row, :], coeff_far[...],
+            (((1,), (1,)), ((), ())), preferred_element_type=jnp.float32,
+        )
+        copies.append(pltpu.make_async_copy(held.at[row], out_hbm.at[y], sems.at[y]))
+        copies[-1].start()
+    for copy in copies:
         copy.wait()
 
 
@@ -323,24 +346,26 @@
     rounds = len(round_plan(nb))
     entries = len(ring_plan(nb)[0])
     share = bands // nz
-    everywhere = pl.BlockSpec(memory_space=pl.ANY)
+    off_chip = pl.BlockSpec(memory_space=pltpu.HBM)
     local = pl.BlockSpec(memory_space=pltpu.VMEM)
     f32, bf16 = jnp.float32, jnp.bfloat16
     dma = pltpu.SemaphoreType.DMA
-    updated, norms = pl.pallas_call(
+    held_bytes = padded * bands * 6 + bands * bands * 2 + 8192
+    held = pl.pallas_call(
         functools.partial(kernel, nb, ny, nz, total_cells),
         out_shape=(
-            jax.ShapeDtypeStruct((rows_y, flat, bands), f32),
-            jax.ShapeDtypeStruct((1, bands), f32),
+            pltpu.VMEM((padded, bands), f32),
+            pltpu.VMEM((padded, bands), bf16),
+            pltpu.VMEM((bands, bands), bf16),
+            pltpu.VMEM((1, bands), f32),
         ),
-        in_specs=[everywhere, everywhere, local, local, local, local],
-        out_specs=(everywhere, local),
+        in_specs=[off_chip, off_chip, local, local, local, local],
+        out_specs=(local, local, local, local),
         scratch_shapes=[
             pltpu.VMEM((rows_y + 2 * REACH, flat, bands), f32),
             pltpu.VMEM((rows_y, flat + 2 * REACH * NX, bands), f32),
             pltpu.VMEM((3, cells, bands), f32),
             pltpu.VMEM((nb, padded, bands), bf16),
-            pltpu.VMEM((padded, bands), f32),
             pltpu.VMEM((bands, padded), bf16),
             pltpu.VMEM((bands, nb * bands), f32),
             pltpu.VMEM((nz, share, nb * bands), f32),
@@ -350,13 +375,24 @@
             pltpu.VMEM((ny, 8, bands), f32),
             dma((3,)), dma((4,)), dma((4,)), dma((2, entries)), dma((2, entries)),
             dma((rounds + 1, 3, max(ny, nz))), dma((rounds + 1, 3, max(ny, nz))),
-            dma((1,)), dma((1,)), dma((rows_y,)),
         ],
         compiler_params=pltpu.CompilerParams(
-            collective_id=0, has_side_effects=True, vmem_limit_bytes=60 * 1024 * 1024
+            collective_id=0, has_side_effects=True, vmem_limit_bytes=67043328 - held_bytes
         ),
         name="sternheimer",
     )(psi, occ, eigen.reshape(1, bands), potential, perturbation, precondition)
+    updated, norms = pl.pallas_call(
+        far_correction,
+        out_shape=(
+            jax.ShapeDtypeStruct((rows_y, flat, bands), f32),
+            jax.ShapeDtypeStruct((1, bands), f32),
+        ),
+        in_specs=[local] * 4,
+        out_specs=(off_chip, local),
+        scratch_shapes=[pltpu.VMEM((cells, bands), f32), dma((rows_y,))],
+        compiler_params=pltpu.CompilerParams(vmem_limit_bytes=16 * 1024 * 1024),
+        name="far_correction",
+    )(*held)
     return jnp.transpose(updated, (2, 0, 1)), norms.reshape(bands)
 
 

time: 96 us -> 93.3 us (0.972)
  local copies, waits for them, and re-layouts: 3.09 us -> 0 us
    unnamed x4 -> x0, local copies, waits for them, and re-layouts: 3.09 us -> none
    pallas_call x0 -> x1, Pallas kernels: none -> 1.89 us  [on_device(): pl.pallas_call(far_correction, out_shape=(jax.ShapeDtypeStruct((rows_y, f...]
    pallas_call x1, Pallas kernels: 92 us -> 90.5 us  [on_device(): pl.pallas_call(functools.partial(kernel, nb, ny, nz, total_cells), out_sh...]
where the time goes in v2:
time: 93.3 us; the launch traced here: 93 us
  Pallas kernels  92.4 us (99%)
    pallas_call x1, Pallas kernels, on_device(): pl.pallas_call(functools.partial(kernel, nb, ny, nz, total_cells), out_sh...  90.5 us
    pallas_call x1, Pallas kernels, on_device(): pl.pallas_call(far_correction, out_shape=(jax.ShapeDtypeStruct((rows_y, f...  1.89 us

profile of v2, /device:TPU:1, one launch (start us, length us, event | category | flops | bytes accessed | tf_op | source)
XLA Modules:
  0.0 93.0 jit_solution(4515828404027816111)
XLA Ops:
  0.6 90.5 %sternheimer.1 = (f32[2944,128]{1,0:T(8,128)S(1)}, bf16[2944,128]{1,0:T(8,128)(2,1)S(1)}, bf16[128,128]{1,0:T(8,128)(2,1)S(1)}, f32[1,128]{1,0:T(1,128)S(1)}) custom-call(f32[6,480,128]{2,1,0:T(8,128)} %bitcast.7, bf16[2880,128]{1,0:T(8,128)(2,1)} %bitcast.8, f32[1,128]{1,0:T(1,128)} %bitcast.9, f32[6,480]{1,0:T(8,128)} %pot_ref.1, f32[6,480]{1,0:T(8,128)} %per_ref.1, ...), custom_call_target="tpu_custom_call" | custom-call | tf_op jit(solution)/shard_map/sternheimer/pallas_call | solution.py:354
  91.1 1.9 %far_correction.1 = (f32[6,480,128]{2,1,0:T(8,128)}, f32[1,128]{1,0:T(1,128)}) custom-call(f32[2944,128]{1,0:T(8,128)S(1)} %get-tuple-element.8.trial, bf16[2944,128]{1,0:T(8,128)(2,1)S(1)} %get-tuple-element.9.occ_far, bf16[128,128]{1,0:T(8,128)(2,1)S(1)} %get-tuple-element.10.coeff_far, f32[1,128]{1,0:T(1,128)S(1)} %get-tuple-element.11.norm_ref), custom_call_target="tpu_custom_call" | custom-call | tf_op jit(solution)/shard_map/far_correction/pallas_call | solution.py:384

commit v3 on v2

--- a/solution.py
+++ b/solution.py
@@ -258,11 +258,9 @@
         for at in range(1, ny):
             total += gyb[at, :, cols]
         mine = pl.ds(pl.multiple_of(my_z * share, 16), share)
-        coeff[mine, cols] = (total / total_cells).astype(coeff.dtype)
-        return spread(
-            lambda p: coeff.at[mine, cols], lambda p: coeff.at[mine, cols],
-            (r, 2), "gz", my_z, nz,
-        )
+        rows = coeff_far.at[mine] if r == last - 1 else coeff.at[mine, cols]
+        rows[...] = (total / total_cells).astype(coeff.dtype)
+        return spread(lambda p: rows, lambda p: rows, (r, 2), "gz", my_z, nz)
 
     def correct(r, copies):
         arrive(copies)
@@ -280,10 +278,17 @@
 
         lax.fori_loop(0, rows_y, rows, 0)
 
-    before = None
+    def settle(copies):
+        for copy in copies:
+            copy.wait_send()
+
+    flying = None
     for r in range(last):
-        dist = r + 1
-        if r == last - 1:
+        dist, final = r + 1, r == last - 1
+        if r == last - 2 and flying is not None:
+            correct(flying[0], over_z(*flying))
+            flying = None
+        if final:
             advance(4 * r + 1)
             part[:, span_of(r)] = far_margins((0, 2))
         advance(4 * dist)
@@ -297,16 +302,17 @@
             sq_copies = spread(
                 lambda p: sq_y.at[my_y], lambda p: sq_y.at[my_y], (last, 1), "gy", my_y, ny
             )
-        advance(4 * dist + 1)
-        if before is not None:
-            three = over_z(r - 1, before)
-            two = over_y(r, one)
-            advance(4 * dist + 2)
-            correct(r - 1, three)
-        else:
-            two = over_y(r, one)
-        before = two
-    three = over_z(last - 1, before)
+        if final and flying is not None:
+            three = over_z(*flying)
+        if r < last - 2:
+            advance(4 * dist + 1)
+        two = over_y(r, one)
+        if flying is not None:
+            if not final:
+                three = over_z(*flying)
+                advance(4 * dist + 2)
+            correct(flying[0], three)
+        flying = (r, two)
 
     arrive(sq_copies)
     over = sq_y[0]
@@ -314,10 +320,11 @@
         over += sq_y[at]
     norm_ref[...] = jnp.sqrt(jnp.sum(over, axis=0, keepdims=True) / total_cells + 1e-06)
 
+    earlier = list(sends)
+    three = over_z(*flying)
+    settle(earlier)
     arrive(three)
-    coeff_far[...] = coeff[:, span_of(last - 1)]
-    for copy in sends:
-        copy.wait_send()
+    settle(three)
 
 
 def far_correction(trial, occ_far, coeff_far, norm_ref, out_hbm, norm_out, held, sems):

time: 93.3 us -> 90.5 us (0.970)
  Pallas kernels: 92.4 us -> 89.6 us
    pallas_call x1, Pallas kernels: 90.5 us -> 87.7 us  [on_device(): pl.pallas_call(functools.partial(kernel, nb, ny, nz, total_cells), out_sh...]
where the time goes in v3:
time: 90.5 us; the launch traced here: 90.2 us
  Pallas kernels  89.6 us (99%)
    pallas_call x1, Pallas kernels, on_device(): pl.pallas_call(functools.partial(kernel, nb, ny, nz, total_cells), out_sh...  87.7 us
    pallas_call x1, Pallas kernels, on_device(): pl.pallas_call(far_correction, out_shape=(jax.ShapeDtypeStruct((rows_y, f...  1.89 us

profile of v3, /device:TPU:1, one launch (start us, length us, event | category | flops | bytes accessed | tf_op | source)
XLA Modules:
  0.0 90.2 jit_solution(8215455161936007919)
XLA Ops:
  0.6 87.7 %sternheimer.1 = (f32[2944,128]{1,0:T(8,128)S(1)}, bf16[2944,128]{1,0:T(8,128)(2,1)S(1)}, bf16[128,128]{1,0:T(8,128)(2,1)S(1)}, f32[1,128]{1,0:T(1,128)S(1)}) custom-call(f32[6,480,128]{2,1,0:T(8,128)} %bitcast.7, bf16[2880,128]{1,0:T(8,128)(2,1)} %bitcast.8, f32[1,128]{1,0:T(1,128)} %bitcast.9, f32[6,480]{1,0:T(8,128)} %pot_ref.1, f32[6,480]{1,0:T(8,128)} %per_ref.1, ...), custom_call_target="tpu_custom_call" | custom-call | tf_op jit(solution)/shard_map/sternheimer/pallas_call | solution.py:361
  88.3 1.9 %far_correction.1 = (f32[6,480,128]{2,1,0:T(8,128)}, f32[1,128]{1,0:T(1,128)}) custom-call(f32[2944,128]{1,0:T(8,128)S(1)} %get-tuple-element.8.trial, bf16[2944,128]{1,0:T(8,128)(2,1)S(1)} %get-tuple-element.9.occ_far, bf16[128,128]{1,0:T(8,128)(2,1)S(1)} %get-tuple-element.10.coeff_far, f32[1,128]{1,0:T(1,128)S(1)} %get-tuple-element.11.norm_ref), custom_call_target="tpu_custom_call" | custom-call | tf_op jit(solution)/shard_map/far_correction/pallas_call | solution.py:391

commit v4 on v3

--- a/solution.py
+++ b/solution.py
@@ -32,14 +32,14 @@
 
 
 def quarters(cells):
-    return [(cells * i // 4 + 64) // 128 * 128 for i in range(4)] + [cells]
+    return [0, (cells // 4 + 64) // 128 * 128, cells // 2, (cells * 3 // 4 + 64) // 128 * 128, cells]
 
 
 def kernel(
     nb, ny, nz, total_cells,
-    psi_hbm, occ_hbm, eig_ref, pot_ref, per_ref, pre_ref,
+    psi_hbm, occ_hbm, eig_hbm, pot_hbm, per_hbm, pre_hbm,
     trial, occ_far, coeff_far, norm_ref,
-    py, pz, fields, occ, low_t, part, rs, gyb, coeff, sq_z, sq_y,
+    eig_ref, grids, py, pz, fields, occ, low_t, part, rs, gyb, coeff, sq_z, sq_y,
     load_sem, halo_send, halo_recv, ring_send, ring_recv, red_send, red_recv,
 ):
     rows_y, flat, bands = psi_hbm.shape
@@ -78,7 +78,16 @@
         pltpu.make_async_copy(psi_hbm, py.at[pl.ds(REACH, rows_y)], load_sem.at[1]),
         pltpu.make_async_copy(psi_hbm, pz.at[:, pl.ds(wide, flat)], load_sem.at[2]),
     ]
-    for load in loads:
+    small = [
+        pltpu.make_async_copy(src, dst, load_sem.at[3 + i])
+        for i, (src, dst) in enumerate(
+            (
+                (pot_hbm, grids.at[0]), (per_hbm, grids.at[1]), (pre_hbm, grids.at[2]),
+                (eig_hbm, eig_ref),
+            )
+        )
+    ]
+    for load in loads + small:
         load.start()
     pl.semaphore_wait(barrier, greeted)
 
@@ -139,8 +148,10 @@
         for at in range(nb):
             occ[at, cells:, :] = jnp.zeros((padded - cells, bands), occ.dtype)
         trial[cells:, :] = jnp.zeros((padded - cells, bands), trial.dtype)
-    for at, ref in enumerate((pot_ref, per_ref, pre_ref)):
-        columns = jnp.transpose(ref[...])
+    for load in small:
+        load.wait()
+    for at in range(3):
+        columns = jnp.transpose(grids[at])
         for y in range(rows_y):
             fields[at, y * flat : (y + 1) * flat, :] = jnp.broadcast_to(
                 columns[:, y : y + 1], (flat, bands)
@@ -212,10 +223,12 @@
     def span_of(r):
         return pl.ds(starts[r], starts[r + 1] - starts[r])
 
+    tiles = [bounds[0], bounds[1], -(-bounds[2] // 128) * 128, bounds[3], padded]
+
     def far_margins(chunks):
         total = 0.0
         for c in chunks:
-            span = pl.ds(bounds[c], (padded if c == 3 else bounds[c + 1]) - bounds[c])
+            span = pl.ds(tiles[c], tiles[c + 1] - tiles[c])
             total += jnp.dot(
                 low_t[:, span], occ_far[span, :], preferred_element_type=jnp.float32
             )
@@ -302,14 +315,12 @@
             sq_copies = spread(
                 lambda p: sq_y.at[my_y], lambda p: sq_y.at[my_y], (last, 1), "gy", my_y, ny
             )
-        if final and flying is not None:
-            three = over_z(*flying)
-        if r < last - 2:
-            advance(4 * dist + 1)
+        if not final:
+            advance(4 * dist + 1 if r < last - 2 else 0)
         two = over_y(r, one)
         if flying is not None:
+            three = over_z(*flying)
             if not final:
-                three = over_z(*flying)
                 advance(4 * dist + 2)
             correct(flying[0], three)
         flying = (r, two)
@@ -329,8 +340,8 @@
 
 def far_correction(trial, occ_far, coeff_far, norm_ref, out_hbm, norm_out, held, sems):
     rows_y, flat, bands = out_hbm.shape
-    norm_out[...] = norm_ref[...]
-    copies = []
+    copies = [pltpu.make_async_copy(norm_ref, norm_out, sems.at[rows_y])]
+    copies[0].start()
     for y in range(rows_y):
         row = pl.ds(y * flat, flat)
         held[row, :] = trial[row, :] - lax.dot_general(
@@ -366,9 +377,11 @@
             pltpu.VMEM((bands, bands), bf16),
             pltpu.VMEM((1, bands), f32),
         ),
-        in_specs=[off_chip, off_chip, local, local, local, local],
+        in_specs=[off_chip] * 6,
         out_specs=(local, local, local, local),
         scratch_shapes=[
+            pltpu.VMEM((1, bands), f32),
+            pltpu.VMEM((3, rows_y, flat), f32),
             pltpu.VMEM((rows_y + 2 * REACH, flat, bands), f32),
             pltpu.VMEM((rows_y, flat + 2 * REACH * NX, bands), f32),
             pltpu.VMEM((3, cells, bands), f32),
@@ -380,7 +393,7 @@
             pltpu.VMEM((bands, nb * bands), bf16),
             pltpu.VMEM((nz, 8, bands), f32),
             pltpu.VMEM((ny, 8, bands), f32),
-            dma((3,)), dma((4,)), dma((4,)), dma((2, entries)), dma((2, entries)),
+            dma((7,)), dma((4,)), dma((4,)), dma((2, entries)), dma((2, entries)),
             dma((rounds + 1, 3, max(ny, nz))), dma((rounds + 1, 3, max(ny, nz))),
         ],
         compiler_params=pltpu.CompilerParams(
@@ -395,8 +408,8 @@
             jax.ShapeDtypeStruct((1, bands), f32),
         ),
         in_specs=[local] * 4,
-        out_specs=(off_chip, local),
-        scratch_shapes=[pltpu.VMEM((cells, bands), f32), dma((rows_y,))],
+        out_specs=(off_chip, off_chip),
+        scratch_shapes=[pltpu.VMEM((cells, bands), f32), dma((rows_y + 1,))],
         compiler_params=pltpu.CompilerParams(vmem_limit_bytes=16 * 1024 * 1024),
         name="far_correction",
     )(*held)

time: 90.5 us -> 89.3 us (0.987)
  Pallas kernels: 89.6 us -> 88.6 us
where the time goes in v4:
time: 89.3 us; the launch traced here: 89.2 us
  Pallas kernels  88.6 us (99%)
    pallas_call x1, Pallas kernels, on_device(): pl.pallas_call(functools.partial(kernel, nb, ny, nz, total_cells), out_sh...  87.2 us

profile of v4, /device:TPU:1, one launch (start us, length us, event | category | flops | bytes accessed | tf_op | source)
XLA Modules:
  0.0 89.2 jit_solution(3096562161124181227)
XLA Ops:
  0.6 87.2 %sternheimer.1 = (f32[2944,128]{1,0:T(8,128)S(1)}, bf16[2944,128]{1,0:T(8,128)(2,1)S(1)}, bf16[128,128]{1,0:T(8,128)(2,1)S(1)}, f32[1,128]{1,0:T(1,128)S(1)}) custom-call(f32[6,480,128]{2,1,0:T(8,128)} %bitcast.7, bf16[2880,128]{1,0:T(8,128)(2,1)} %bitcast.8, f32[1,128]{1,0:T(1,128)} %bitcast.9, f32[6,480]{1,0:T(8,128)} %pot_hbm.1, f32[6,480]{1,0:T(8,128)} %per_hbm.1, ...), custom_call_target="tpu_custom_call" | custom-call | tf_op jit(solution)/shard_map/sternheimer/pallas_call | solution.py:372
  87.8 1.4 %far_correction.1 = (f32[6,480,128]{2,1,0:T(8,128)}, f32[1,128]{1,0:T(1,128)}) custom-call(f32[2944,128]{1,0:T(8,128)S(1)} %get-tuple-element.8.trial, bf16[2944,128]{1,0:T(8,128)(2,1)S(1)} %get-tuple-element.9.occ_far, bf16[128,128]{1,0:T(8,128)(2,1)S(1)} %get-tuple-element.10.coeff_far, f32[1,128]{1,0:T(1,128)S(1)} %get-tuple-element.11.norm_ref), custom_call_target="tpu_custom_call" | custom-call | tf_op jit(solution)/shard_map/far_correction/pallas_call | solution.py:404

commit v5 on v4

--- a/solution.py
+++ b/solution.py
@@ -39,7 +39,8 @@
     nb, ny, nz, total_cells,
     psi_hbm, occ_hbm, eig_hbm, pot_hbm, per_hbm, pre_hbm,
     trial, occ_far, coeff_far, norm_ref,
-    eig_ref, grids, py, pz, fields, occ, low_t, part, rs, gyb, coeff, sq_z, sq_y,
+    eig_ref, grids, py, pz, fields, occ, low_t, part, rs, gyb,
+    coeff, sq_z, sq_y,
     load_sem, halo_send, halo_recv, ring_send, ring_recv, red_send, red_recv,
 ):
     rows_y, flat, bands = psi_hbm.shape
@@ -234,42 +235,45 @@
             )
         return total
 
+    def buffers(r):
+        cols = span_of(r)
+        return part.at[:, cols], rs.at[:, :, cols], gyb.at[:, :, cols]
+
     def margins(r):
-        cols = span_of(r)
+        sums, slots, _ = buffers(r)
         if r == last - 1:
-            part[:, cols] += far_margins((1, 3))
+            sums[...] += far_margins((1, 3))
         else:
             for i, at in enumerate(rounds[r]):
-                part[:, pl.ds(starts[r] + i * bands, bands)] = jnp.dot(
+                sums[:, i * bands : (i + 1) * bands] = jnp.dot(
                     low_t[...], occ[at], preferred_element_type=jnp.float32
                 )
-        mine = pl.ds(pl.multiple_of(my_z * share, 16), share)
         copies = spread(
-            lambda p: part.at[pl.ds(pl.multiple_of(p * share, 16), share), cols],
-            lambda p: rs.at[my_z, :, cols],
+            lambda p: sums.at[pl.ds(pl.multiple_of(p * share, 16), share)],
+            lambda p: slots.at[my_z],
             (r, 0), "gz", my_z, nz,
         )
-        rs[my_z, :, cols] = part[mine, cols]
+        slots[my_z] = sums[pl.ds(pl.multiple_of(my_z * share, 16), share), :]
         return copies
+
+    def summed(slots, count):
+        total = slots[0]
+        for at in range(1, count):
+            total += slots[at]
+        return total
 
     def over_y(r, copies):
         arrive(copies)
-        cols = span_of(r)
-        total = rs[0, :, cols]
-        for at in range(1, nz):
-            total += rs[at, :, cols]
-        gyb[my_y, :, cols] = total
+        _, slots, shares = buffers(r)
+        shares[my_y] = summed(slots, nz)
         return spread(
-            lambda p: gyb.at[my_y, :, cols], lambda p: gyb.at[my_y, :, cols],
-            (r, 1), "gy", my_y, ny,
+            lambda p: shares.at[my_y], lambda p: shares.at[my_y], (r, 1), "gy", my_y, ny
         )
 
     def over_z(r, copies):
         arrive(copies)
         cols = span_of(r)
-        total = gyb[0, :, cols]
-        for at in range(1, ny):
-            total += gyb[at, :, cols]
+        total = summed(buffers(r)[2], ny)
         mine = pl.ds(pl.multiple_of(my_z * share, 16), share)
         rows = coeff_far.at[mine] if r == last - 1 else coeff.at[mine, cols]
         rows[...] = (total / total_cells).astype(coeff.dtype)
@@ -298,8 +302,9 @@
     flying = None
     for r in range(last):
         dist, final = r + 1, r == last - 1
+        ending = None
         if r == last - 2 and flying is not None:
-            correct(flying[0], over_z(*flying))
+            ending = (flying[0], over_z(*flying))
             flying = None
         if final:
             advance(4 * r + 1)
@@ -315,14 +320,16 @@
             sq_copies = spread(
                 lambda p: sq_y.at[my_y], lambda p: sq_y.at[my_y], (last, 1), "gy", my_y, ny
             )
-        if not final:
-            advance(4 * dist + 1 if r < last - 2 else 0)
+        if ending is not None:
+            correct(*ending)
+        if r < last - 2:
+            advance(4 * dist + 1)
         two = over_y(r, one)
         if flying is not None:
-            three = over_z(*flying)
+            ending = (flying[0], over_z(*flying))
             if not final:
                 advance(4 * dist + 2)
-            correct(flying[0], three)
+                correct(*ending)
         flying = (r, two)
 
     arrive(sq_copies)
@@ -333,6 +340,8 @@
 
     earlier = list(sends)
     three = over_z(*flying)
+    if ending is not None:
+        correct(*ending)
     settle(earlier)
     arrive(three)
     settle(three)

time: 89.3 us -> 88.6 us (level)
  no operation moved by 1% of the time
where the time goes in v5:
time: 88.6 us; the launch traced here: 88.5 us
  Pallas kernels  87.8 us (99%)
    pallas_call x1, Pallas kernels, on_device(): pl.pallas_call(functools.partial(kernel, nb, ny, nz, total_cells), out_sh...  86.4 us

profile of v5, /device:TPU:1, one launch (start us, length us, event | category | flops | bytes accessed | tf_op | source)
XLA Modules:
  0.0 88.5 jit_solution(14058699887783117457)
XLA Ops:
  0.6 86.4 %sternheimer.1 = (f32[2944,128]{1,0:T(8,128)S(1)}, bf16[2944,128]{1,0:T(8,128)(2,1)S(1)}, bf16[128,128]{1,0:T(8,128)(2,1)S(1)}, f32[1,128]{1,0:T(1,128)S(1)}) custom-call(f32[6,480,128]{2,1,0:T(8,128)} %bitcast.7, bf16[2880,128]{1,0:T(8,128)(2,1)} %bitcast.8, f32[1,128]{1,0:T(1,128)} %bitcast.9, f32[6,480]{1,0:T(8,128)} %pot_hbm.1, f32[6,480]{1,0:T(8,128)} %per_hbm.1, ...), custom_call_target="tpu_custom_call" | custom-call | tf_op jit(solution)/shard_map/sternheimer/pallas_call | solution.py:381
  87.1 1.4 %far_correction.1 = (f32[6,480,128]{2,1,0:T(8,128)}, f32[1,128]{1,0:T(1,128)}) custom-call(f32[2944,128]{1,0:T(8,128)S(1)} %get-tuple-element.8.trial, bf16[2944,128]{1,0:T(8,128)(2,1)S(1)} %get-tuple-element.9.occ_far, bf16[128,128]{1,0:T(8,128)(2,1)S(1)} %get-tuple-element.10.coeff_far, f32[1,128]{1,0:T(1,128)S(1)} %get-tuple-element.11.norm_ref), custom_call_target="tpu_custom_call" | custom-call | tf_op jit(solution)/shard_map/far_correction/pallas_call | solution.py:413

commit v6 on v5

--- a/solution.py
+++ b/solution.py
@@ -41,7 +41,7 @@
     trial, occ_far, coeff_far, norm_ref,
     eig_ref, grids, py, pz, fields, occ, low_t, part, rs, gyb,
     coeff, sq_z, sq_y,
-    load_sem, halo_send, halo_recv, ring_send, ring_recv, red_send, red_recv,
+    load_sem, halo_send, halo_recv, ring_send, ring_recv, red_send, red_recv, word,
 ):
     rows_y, flat, bands = psi_hbm.shape
     rows_z = flat // NX
@@ -66,8 +66,8 @@
     greeted = 0
     for axis, me, count, steps in (
         ("band", my_b, nb, (1, nb - 1)),
-        ("gy", my_y, ny, range(1, ny)),
-        ("gz", my_z, nz, range(1, nz)),
+        ("gy", my_y, ny, (1, ny - 1)),
+        ("gz", my_z, nz, (1, nz - 1)),
     ):
         for step in steps:
             pl.semaphore_signal(
@@ -132,6 +132,21 @@
         remote(psi_hbm.at[:, pl.ds(0, wide)], pz.at[:, pl.ds(wide + flat, wide)],
                halo_send.at[3], halo_recv.at[3], gz=z_down),
     ]
+
+    for wave in range(max(ny, nz) // 2 - 1):
+        lines = [
+            (axis, at, ups)
+            for axis, at, ups, count in (("gy", 0, (y_up, y_down), ny), ("gz", 1, (z_up, z_down), nz))
+            if wave < count // 2 - 1
+        ]
+        for axis, at, ups in lines:
+            for way in range(2):
+                pl.semaphore_signal(
+                    word.at[at, wave, way], inc=1, device_id={axis: ups[way]}, device_id_type=MESH
+                )
+        for _, at, _ in lines:
+            for way in range(2):
+                pl.semaphore_wait(word.at[at, wave, way], 1)
 
     arrived = 0
 
@@ -404,6 +419,7 @@
             pltpu.VMEM((ny, 8, bands), f32),
             dma((7,)), dma((4,)), dma((4,)), dma((2, entries)), dma((2, entries)),
             dma((rounds + 1, 3, max(ny, nz))), dma((rounds + 1, 3, max(ny, nz))),
+            pltpu.SemaphoreType.REGULAR((2, max(max(ny, nz) // 2 - 1, 1), 2)),
         ],
         compiler_params=pltpu.CompilerParams(
             collective_id=0, has_side_effects=True, vmem_limit_bytes=67043328 - held_bytes

time: 88.6 us -> 87.3 us (0.985)
  Pallas kernels: 87.8 us -> 86.6 us
    pallas_call x1, Pallas kernels: 86.4 us -> 85.2 us  [on_device(): pl.pallas_call(functools.partial(kernel, nb, ny, nz, total_cells), out_sh...]
where the time goes in v6:
time: 87.3 us; the launch traced here: 87.2 us
  Pallas kernels  86.6 us (99%)
    pallas_call x1, Pallas kernels, on_device(): pl.pallas_call(functools.partial(kernel, nb, ny, nz, total_cells), out_sh...  85.2 us

profile of v6, /device:TPU:1, one launch (start us, length us, event | category | flops | bytes accessed | tf_op | source)
XLA Modules:
  0.0 87.2 jit_solution(8862638229958574320)
XLA Ops:
  0.6 85.2 %sternheimer.1 = (f32[2944,128]{1,0:T(8,128)S(1)}, bf16[2944,128]{1,0:T(8,128)(2,1)S(1)}, bf16[128,128]{1,0:T(8,128)(2,1)S(1)}, f32[1,128]{1,0:T(1,128)S(1)}) custom-call(f32[6,480,128]{2,1,0:T(8,128)} %bitcast.7, bf16[2880,128]{1,0:T(8,128)(2,1)} %bitcast.8, f32[1,128]{1,0:T(1,128)} %bitcast.9, f32[6,480]{1,0:T(8,128)} %pot_hbm.1, f32[6,480]{1,0:T(8,128)} %per_hbm.1, ...), custom_call_target="tpu_custom_call" | custom-call | tf_op jit(solution)/shard_map/sternheimer/pallas_call | solution.py:396
  85.8 1.4 %far_correction.1 = (f32[6,480,128]{2,1,0:T(8,128)}, f32[1,128]{1,0:T(1,128)}) custom-call(f32[2944,128]{1,0:T(8,128)S(1)} %get-tuple-element.8.trial, bf16[2944,128]{1,0:T(8,128)(2,1)S(1)} %get-tuple-element.9.occ_far, bf16[128,128]{1,0:T(8,128)(2,1)S(1)} %get-tuple-element.10.coeff_far, f32[1,128]{1,0:T(1,128)S(1)} %get-tuple-element.11.norm_ref), custom_call_target="tpu_custom_call" | custom-call | tf_op jit(solution)/shard_map/far_correction/pallas_call | solution.py:429

commit v7 on v6

--- a/solution.py
+++ b/solution.py
@@ -88,8 +88,6 @@
             )
         )
     ]
-    for load in loads + small:
-        load.start()
     pl.semaphore_wait(barrier, greeted)
 
     plans = ring_plan(nb)
@@ -132,6 +130,9 @@
         remote(psi_hbm.at[:, pl.ds(0, wide)], pz.at[:, pl.ds(wide + flat, wide)],
                halo_send.at[3], halo_recv.at[3], gz=z_down),
     ]
+
+    for load in small + loads:
+        load.start()
 
     for wave in range(max(ny, nz) // 2 - 1):
         lines = [
@@ -223,7 +224,7 @@
 
     last = len(round_plan(nb))
     sq_z[my_z] = squares
-    sq_copies = spread(lambda p: sq_z.at[my_z], lambda p: sq_z.at[my_z], (last, 0), "gz", my_z, nz)
+    sq_copies = spread(lambda p: sq_z.at[my_z], lambda p: sq_z.at[my_z], (last + 1, 0), "gz", my_z, nz)
 
     for at in range(padded // 128):
         block = pl.ds(at * 128, 128)
@@ -249,6 +250,11 @@
                 low_t[:, span], occ_far[span, :], preferred_element_type=jnp.float32
             )
         return total
+
+    def pieces(r):
+        if r == last - 1:
+            return ((0, share // 2), (share // 2, share // 2))
+        return ((0, share),)
 
     def buffers(r):
         cols = span_of(r)
@@ -263,36 +269,49 @@
                 sums[:, i * bands : (i + 1) * bands] = jnp.dot(
                     low_t[...], occ[at], preferred_element_type=jnp.float32
                 )
-        copies = spread(
-            lambda p: sums.at[pl.ds(pl.multiple_of(p * share, 16), share)],
-            lambda p: slots.at[my_z],
-            (r, 0), "gz", my_z, nz,
-        )
+        copies = [
+            spread(
+                lambda p: sums.at[pl.ds(pl.multiple_of(p * share + low, count), count)],
+                lambda p: slots.at[my_z, pl.ds(low, count)],
+                (r + i, 0), "gz", my_z, nz,
+            )
+            for i, (low, count) in enumerate(pieces(r))
+        ]
         slots[my_z] = sums[pl.ds(pl.multiple_of(my_z * share, 16), share), :]
         return copies
 
-    def summed(slots, count):
-        total = slots[0]
+    def summed(slots, count, rows):
+        total = slots[0, rows, :]
         for at in range(1, count):
-            total += slots[at]
+            total += slots[at, rows, :]
         return total
 
     def over_y(r, copies):
-        arrive(copies)
         _, slots, shares = buffers(r)
-        shares[my_y] = summed(slots, nz)
-        return spread(
-            lambda p: shares.at[my_y], lambda p: shares.at[my_y], (r, 1), "gy", my_y, ny
-        )
+        out = []
+        for i, (low, count) in enumerate(pieces(r)):
+            rows = pl.ds(low, count)
+            arrive(copies[i])
+            shares[my_y, rows, :] = summed(slots, nz, rows)
+            out.append(
+                spread(
+                    lambda p: shares.at[my_y, rows], lambda p: shares.at[my_y, rows],
+                    (r + i, 1), "gy", my_y, ny,
+                )
+            )
+        return out
 
     def over_z(r, copies):
-        arrive(copies)
         cols = span_of(r)
-        total = summed(buffers(r)[2], ny)
-        mine = pl.ds(pl.multiple_of(my_z * share, 16), share)
-        rows = coeff_far.at[mine] if r == last - 1 else coeff.at[mine, cols]
-        rows[...] = (total / total_cells).astype(coeff.dtype)
-        return spread(lambda p: rows, lambda p: rows, (r, 2), "gz", my_z, nz)
+        out = []
+        for i, (low, count) in enumerate(pieces(r)):
+            arrive(copies[i])
+            total = summed(buffers(r)[2], ny, pl.ds(low, count))
+            mine = pl.ds(pl.multiple_of(my_z * share + low, count), count)
+            rows = coeff_far.at[mine] if r == last - 1 else coeff.at[mine, cols]
+            rows[...] = (total / total_cells).astype(coeff.dtype)
+            out += spread(lambda p: rows, lambda p: rows, (r + i, 2), "gz", my_z, nz)
+        return out
 
     def correct(r, copies):
         arrive(copies)
@@ -333,7 +352,7 @@
                 over += sq_z[at]
             sq_y[my_y] = over
             sq_copies = spread(
-                lambda p: sq_y.at[my_y], lambda p: sq_y.at[my_y], (last, 1), "gy", my_y, ny
+                lambda p: sq_y.at[my_y], lambda p: sq_y.at[my_y], (last + 1, 1), "gy", my_y, ny
             )
         if ending is not None:
             correct(*ending)
@@ -418,7 +437,7 @@
             pltpu.VMEM((nz, 8, bands), f32),
             pltpu.VMEM((ny, 8, bands), f32),
             dma((7,)), dma((4,)), dma((4,)), dma((2, entries)), dma((2, entries)),
-            dma((rounds + 1, 3, max(ny, nz))), dma((rounds + 1, 3, max(ny, nz))),
+            dma((rounds + 2, 3, max(ny, nz))), dma((rounds + 2, 3, max(ny, nz))),
             pltpu.SemaphoreType.REGULAR((2, max(max(ny, nz) // 2 - 1, 1), 2)),
         ],
         compiler_params=pltpu.CompilerParams(

time: 87.3 us -> 87.8 us (level)
  no operation moved by 1% of the time
where the time goes in v7:
time: 87.8 us; the launch traced here: 87.6 us
  Pallas kernels  87 us (99%)
    pallas_call x1, Pallas kernels, on_device(): pl.pallas_call(functools.partial(kernel, nb, ny, nz, total_cells), out_sh...  85.6 us

profile of v7, /device:TPU:1, one launch (start us, length us, event | category | flops | bytes accessed | tf_op | source)
XLA Modules:
  0.0 87.6 jit_solution(16360524074161149258)
XLA Ops:
  0.6 85.6 %sternheimer.1 = (f32[2944,128]{1,0:T(8,128)S(1)}, bf16[2944,128]{1,0:T(8,128)(2,1)S(1)}, bf16[128,128]{1,0:T(8,128)(2,1)S(1)}, f32[1,128]{1,0:T(1,128)S(1)}) custom-call(f32[6,480,128]{2,1,0:T(8,128)} %bitcast.7, bf16[2880,128]{1,0:T(8,128)(2,1)} %bitcast.8, f32[1,128]{1,0:T(1,128)} %bitcast.9, f32[6,480]{1,0:T(8,128)} %pot_hbm.1, f32[6,480]{1,0:T(8,128)} %per_hbm.1, ...), custom_call_target="tpu_custom_call" | custom-call | tf_op jit(solution)/shard_map/sternheimer/pallas_call | solution.py:415
  86.3 1.4 %far_correction.1 = (f32[6,480,128]{2,1,0:T(8,128)}, f32[1,128]{1,0:T(1,128)}) custom-call(f32[2944,128]{1,0:T(8,128)S(1)} %get-tuple-element.8.trial, bf16[2944,128]{1,0:T(8,128)(2,1)S(1)} %get-tuple-element.9.occ_far, bf16[128,128]{1,0:T(8,128)(2,1)S(1)} %get-tuple-element.10.coeff_far, f32[1,128]{1,0:T(1,128)S(1)} %get-tuple-element.11.norm_ref), custom_call_target="tpu_custom_call" | custom-call | tf_op jit(solution)/shard_map/far_correction/pallas_call | solution.py:448

commit v8 on v6

--- a/solution.py
+++ b/solution.py
@@ -353,11 +353,10 @@
         over += sq_y[at]
     norm_ref[...] = jnp.sqrt(jnp.sum(over, axis=0, keepdims=True) / total_cells + 1e-06)
 
-    earlier = list(sends)
+    settle(list(sends))
     three = over_z(*flying)
     if ending is not None:
         correct(*ending)
-    settle(earlier)
     arrive(three)
     settle(three)
 

time: 87.3 us -> 87.3 us (level)
  no operation moved by 1% of the time
where the time goes in v8:
time: 87.3 us; the launch traced here: 87.2 us
  Pallas kernels  86.6 us (99%)
    pallas_call x1, Pallas kernels, on_device(): pl.pallas_call(functools.partial(kernel, nb, ny, nz, total_cells), out_sh...  85.2 us

profile of v8, /device:TPU:1, one launch (start us, length us, event | category | flops | bytes accessed | tf_op | source)
XLA Modules:
  0.0 87.2 jit_solution(5767721973131012323)
XLA Ops:
  0.6 85.2 %sternheimer.1 = (f32[2944,128]{1,0:T(8,128)S(1)}, bf16[2944,128]{1,0:T(8,128)(2,1)S(1)}, bf16[128,128]{1,0:T(8,128)(2,1)S(1)}, f32[1,128]{1,0:T(1,128)S(1)}) custom-call(f32[6,480,128]{2,1,0:T(8,128)} %bitcast.7, bf16[2880,128]{1,0:T(8,128)(2,1)} %bitcast.8, f32[1,128]{1,0:T(1,128)} %bitcast.9, f32[6,480]{1,0:T(8,128)} %pot_hbm.1, f32[6,480]{1,0:T(8,128)} %per_hbm.1, ...), custom_call_target="tpu_custom_call" | custom-call | tf_op jit(solution)/shard_map/sternheimer/pallas_call | solution.py:395
  85.8 1.4 %far_correction.1 = (f32[6,480,128]{2,1,0:T(8,128)}, f32[1,128]{1,0:T(1,128)}) custom-call(f32[2944,128]{1,0:T(8,128)S(1)} %get-tuple-element.8.trial, bf16[2944,128]{1,0:T(8,128)(2,1)S(1)} %get-tuple-element.9.occ_far, bf16[128,128]{1,0:T(8,128)(2,1)S(1)} %get-tuple-element.10.coeff_far, f32[1,128]{1,0:T(1,128)S(1)} %get-tuple-element.11.norm_ref), custom_call_target="tpu_custom_call" | custom-call | tf_op jit(solution)/shard_map/far_correction/pallas_call | solution.py:428

commit v9 on v8

--- a/solution.py
+++ b/solution.py
@@ -88,8 +88,6 @@
             )
         )
     ]
-    for load in loads + small:
-        load.start()
     pl.semaphore_wait(barrier, greeted)
 
     plans = ring_plan(nb)
@@ -132,6 +130,9 @@
         remote(psi_hbm.at[:, pl.ds(0, wide)], pz.at[:, pl.ds(wide + flat, wide)],
                halo_send.at[3], halo_recv.at[3], gz=z_down),
     ]
+
+    for load in small + loads:
+        load.start()
 
     for wave in range(max(ny, nz) // 2 - 1):
         lines = [

time: 87.3 us -> 87.3 us (level)
  no operation moved by 1% of the time
where the time goes in v9:
time: 87.3 us; the launch traced here: 87.2 us
  Pallas kernels  86.6 us (99%)
    pallas_call x1, Pallas kernels, on_device(): pl.pallas_call(functools.partial(kernel, nb, ny, nz, total_cells), out_sh...  85.2 us

profile of v9, /device:TPU:1, one launch (start us, length us, event | category | flops | bytes accessed | tf_op | source)
XLA Modules:
  0.0 87.2 jit_solution(8291038141127818945)
XLA Ops:
  0.6 85.2 %sternheimer.1 = (f32[2944,128]{1,0:T(8,128)S(1)}, bf16[2944,128]{1,0:T(8,128)(2,1)S(1)}, bf16[128,128]{1,0:T(8,128)(2,1)S(1)}, f32[1,128]{1,0:T(1,128)S(1)}) custom-call(f32[6,480,128]{2,1,0:T(8,128)} %bitcast.7, bf16[2880,128]{1,0:T(8,128)(2,1)} %bitcast.8, f32[1,128]{1,0:T(1,128)} %bitcast.9, f32[6,480]{1,0:T(8,128)} %pot_hbm.1, f32[6,480]{1,0:T(8,128)} %per_hbm.1, ...), custom_call_target="tpu_custom_call" | custom-call | tf_op jit(solution)/shard_map/sternheimer/pallas_call | solution.py:396
  85.8 1.4 %far_correction.1 = (f32[6,480,128]{2,1,0:T(8,128)}, f32[1,128]{1,0:T(1,128)}) custom-call(f32[2944,128]{1,0:T(8,128)S(1)} %get-tuple-element.8.trial, bf16[2944,128]{1,0:T(8,128)(2,1)S(1)} %get-tuple-element.9.occ_far, bf16[128,128]{1,0:T(8,128)(2,1)S(1)} %get-tuple-element.10.coeff_far, f32[1,128]{1,0:T(1,128)S(1)} %get-tuple-element.11.norm_ref), custom_call_target="tpu_custom_call" | custom-call | tf_op jit(solution)/shard_map/far_correction/pallas_call | solution.py:429
